TPU v7x, 128 devices: a whole 4x4x4 slice. The times are simulated.
128 devices in a mesh: lat: 8 (over y_hi, z), lon: 16 (over x, y_lo, core).
Axes of the slice: x: 4, y: 4 (y_hi: 2, y_lo: 2; y = y_hi * 2 + y_lo), z: 4, core: 2. Of those that a mesh axis runs over, the one named last changes fastest.
Arguments:
- fields: bfloat16 [2, 256, 768, 256], P(None, 'lat', 'lon'), may hold values from -6 to 6
- kernel: bfloat16 [9, 256, 256], replicated, may hold values from -0.125 to 0.125
- conv_bias: float32 [256], replicated, may hold values from -3 to 3
- cotangent: bfloat16 [2, 128, 384, 256], P(None, 'lat', 'lon'), may hold values from -6 to 6
Outputs:
- pooled: bfloat16 [2, 128, 384, 256], P(None, 'lat', 'lon')
- grad_input: bfloat16 [2, 256, 768, 256], P(None, 'lat', 'lon')
- grad_kernel: float32 [9, 256, 256], replicated
- grad_bias: float32 [256], replicated
All inputs are finite; a program needn't handle non-finite values.
Results may differ from a plain program's by a relative error of at most 0.013.
Values may be sent and summed in bfloat16 or wider, within the bound.
No kernel may reach another device: no remote copies, remote signals or barrier semaphores. Data moves between devices by JAX's collectives and lax.ppermute only.
A program may use at most 64 MiB of HBM per device.

v0:
```python
import math
import jax
import jax.numpy as jnp
from jax import lax
from jax.sharding import PartitionSpec as P


def shifted(shard, axis, by):
    size = lax.axis_size(axis)
    return lax.ppermute(shard, axis, [(i, (i + by) % size) for i in range(size)])


def with_halo(shard, sides, width, wrap):
    for axis, dim in sides:
        size, length = (lax.axis_size(axis), shard.shape[dim])
        up = [(i, (i + 1) % size) for i in range(size if wrap else size - 1)]
        down = [(j, i) for i, j in up]
        last = lax.slice_in_dim(shard, length - width, length, axis=dim)
        first = lax.slice_in_dim(shard, 0, width, axis=dim)
        before = lax.ppermute(last, axis, up)
        after = lax.ppermute(first, axis, down)
        shard = jnp.concatenate([before, shard, after], axis=dim)
    return shard


def lat_cosine(rows, first, total):
    index_rows = (first + jnp.arange(rows)).astype(jnp.float32)
    return jnp.cos((index_rows + 0.5) * (math.pi / total) - math.pi / 2)


def extend(field):
    lat_count = lax.axis_size("lat")
    lat_place = lax.axis_index("lat")
    lon_count = lax.axis_size("lon")
    north_row = field[:, :1]
    south_row = field[:, -1:]
    mirror_north, mirror_south = shifted((north_row, south_row), "lon", lon_count // 2)
    rim_rows = with_halo(field, (("lat", 1),), 1, False)
    upper_pad = jnp.where(lat_place == 0, mirror_north, rim_rows[:, :1])
    bottom = jnp.where(lat_place == lat_count - 1, mirror_south, rim_rows[:, -1:])
    tall = jnp.concatenate([upper_pad, field, bottom], axis=1)
    return with_halo(tall, (("lon", 2),), 1, True)


def forward_conv(padded, kernel, rows, cols):
    chans = padded.shape[-1]
    total = jnp.zeros((padded.shape[0] * rows * cols, kernel.shape[2]), jnp.float32)
    for row_off in range(3):
        for col_off in range(3):
            window = padded[:, row_off : row_off + rows, col_off : col_off + cols, :].reshape(
                -1, chans
            )
            total = total + jnp.dot(
                window, kernel[3 * row_off + col_off], preferred_element_type=jnp.float32
            )
    return total.reshape(padded.shape[0], rows, cols, kernel.shape[2])


def back_conv(padded, kernel, rows, cols):
    chans = padded.shape[-1]
    total = jnp.zeros((padded.shape[0] * rows * cols, kernel.shape[1]), jnp.float32)
    for row_off in range(3):
        for col_off in range(3):
            window = padded[
                :, 2 - row_off : 2 - row_off + rows, 2 - col_off : 2 - col_off + cols, :
            ].reshape(-1, chans)
            total = total + lax.dot_general(
                window,
                kernel[3 * row_off + col_off],
                (((1,), (1,)), ((), ())),
                preferred_element_type=jnp.float32,
            )
    return total.reshape(padded.shape[0], rows, cols, kernel.shape[1])


def pole_term(pad_row, kernel, row_off, cols):
    chans = pad_row.shape[-1]
    total = jnp.zeros((pad_row.shape[0] * cols, kernel.shape[1]), jnp.float32)
    for col_off in range(3):
        window = pad_row[:, :, 2 - col_off : 2 - col_off + cols, :].reshape(-1, chans)
        total = total + lax.dot_general(
            window,
            kernel[3 * row_off + col_off],
            (((1,), (1,)), ((), ())),
            preferred_element_type=jnp.float32,
        )
    return total.reshape(pad_row.shape[0], 1, cols, kernel.shape[1])


def kernel_grad(padded, grad_pre, rows, cols):
    chans = padded.shape[-1]
    flat_grad = grad_pre.reshape(-1, grad_pre.shape[-1])
    pieces = []
    for row_off in range(3):
        for col_off in range(3):
            window = padded[:, row_off : row_off + rows, col_off : col_off + cols, :].reshape(
                -1, chans
            )
            pieces.append(
                lax.dot_general(
                    window, flat_grad, (((0,), (0,)), ((), ())), preferred_element_type=jnp.float32
                )
            )
    return jnp.stack(pieces, axis=0)


def local(fields, kernel, conv_bias, cotangent):
    batches, rows, cols, chans = fields.shape
    lat_count = lax.axis_size("lat")
    lat_place = lax.axis_index("lat")
    padded = extend(fields)
    pre = forward_conv(padded, kernel, rows, cols) + conv_bias
    sigma = jax.nn.sigmoid(pre)
    active = (pre * sigma).astype(jnp.bfloat16)
    cosine = lat_cosine(rows, lat_place * rows, rows * lat_count)
    pair_sum = cosine[0::2] + cosine[1::2]
    weighted = active.astype(jnp.float32) * cosine[None, :, None, None]
    pooled = (
        weighted.reshape(batches, rows // 2, 2, cols // 2, 2, chans).sum(axis=(2, 4))
        / (2.0 * pair_sum)[None, :, None, None]
    )
    share = cosine / (2.0 * jnp.repeat(pair_sum, 2))
    spread = jnp.repeat(jnp.repeat(cotangent.astype(jnp.float32), 2, axis=1), 2, axis=2)
    grad_pre = (spread * share[None, :, None, None] * sigma * (1.0 + pre * (1.0 - sigma))).astype(
        jnp.bfloat16
    )
    kernel_part = kernel_grad(padded, grad_pre, rows, cols)
    bias_part = jnp.sum(grad_pre.astype(jnp.float32), axis=(0, 1, 2))
    grad_kernel, grad_bias = lax.psum((kernel_part, bias_part), ("lat", "lon"))
    grad_padded = extend(grad_pre)
    is_north = lat_place == 0
    is_south = lat_place == lat_count - 1
    blank = jnp.zeros_like(grad_padded[:, :1])
    upper_rows = jnp.where(is_north, blank, grad_padded[:, :1])
    lower_rows = jnp.where(is_south, blank, grad_padded[:, -1:])
    inner = jnp.concatenate([upper_rows, grad_padded[:, 1:-1], lower_rows], axis=1)
    back = back_conv(inner, kernel, rows, cols)
    north_add = jnp.where(is_north, pole_term(grad_padded[:, :1], kernel, 0, cols), 0.0)
    south_add = jnp.where(is_south, pole_term(grad_padded[:, -1:], kernel, 2, cols), 0.0)
    back = jnp.concatenate(
        [back[:, :1] + north_add, back[:, 1:-1], back[:, -1:] + south_add], axis=1
    )
    return (pooled.astype(jnp.bfloat16), back.astype(jnp.bfloat16), grad_kernel, grad_bias)


def solution(mesh):
    return jax.shard_map(
        local,
        mesh=mesh,
        in_specs=(P(None, "lat", "lon", None), P(), P(), P(None, "lat", "lon", None)),
        out_specs=(P(None, "lat", "lon", None), P(None, "lat", "lon", None), P(), P()),
        check_vma=False,
    )
```

profile of v0, /device:TPU:1, one launch (start us, length us, event | category | flops | bytes accessed | tf_op | source)
XLA Modules:
  0.0 244.1 jit_solution(9984950914171488139)
XLA Ops:
  8.0 3.6 %collective-permute-start.2 = (bf16[2,1,48,256]{3,2,1,0:T(8,128)(2,1)S(1)}, bf16[2,1,48,256]{3,2,1,0:T(8,128)(2,1)S(1)}, u32[]{:S(2)}, u32[]{:S(2)}) collective-permute-start(bf16[2,1,48,256]{3,2,1,0:T(8,128)(2,1)S(1)} %get-tuple-element.41), channel_id=1, source_target_pairs={{0,8},{1,9},{2,10},{3,11},{4,12},{5,13},{6,14},{7,15},{8,0},{9,1},... | collective-permute-start | bytes 147464 | tf_op jit(solution)/shard_map/ppermute | solution.py:10
  11.7 3.5 %collective-permute-start.1 = (bf16[2,1,48,256]{3,2,1,0:T(8,128)(2,1)S(1)}, bf16[2,1,48,256]{3,2,1,0:T(8,128)(2,1)S(1)}, u32[]{:S(2)}, u32[]{:S(2)}) collective-permute-start(bf16[2,1,48,256]{3,2,1,0:T(8,128)(2,1)S(1)} %get-tuple-element.41), channel_id=1, source_target_pairs={{0,16},{16,32},{32,48},{48,64},{64,80},{80,96},{96,112},{1,17},{17... | collective-permute-start | bytes 147464 | tf_op jit(solution)/shard_map/ppermute | solution.py:20
  18.5 1.7 broadcast_in_dim.22
  20.3 3.4 %reshape.184 = f32[3072,256]{1,0:T(8,128)} reshape(f32[2,32,24,2,256]{4,3,2,1,0:T(2,128)S(1)} %broadcast_in_dim.22) | data formatting | bytes 6291456 | tf_op jit(solution)/shard_map/reshape | solution.py:123
  23.7 3.4 %reshape.178 = f32[2,32,48,256]{3,2,1,0:T(8,128)} reshape(f32[2,32,24,2,256]{4,3,2,1,0:T(2,128)S(1)} %broadcast_in_dim.22) | data formatting | bytes 6291456 | tf_op jit(solution)/shard_map/reshape | solution.py:123
  28.8 1.6 collective-permute-start.5
  30.4 1.4 collective-permute-start.4
  34.9 3.1 %fusion.104 = (bf16[2,32,48,256]{3,2,1,0:T(8,128)(2,1)S(1)}, bf16[2,32,48,256]{3,2,1,0:T(8,128)(2,1)S(1)}, bf16[2,32,48,256]{3,2,1,0:T(8,128)(2,1)S(1)}, bf16[2,...) fusion(bf16[2,34,49,256]{3,2,1,0:T(8,128)(2,1)S(1)} %get-tuple-element., ...), kind=kLoop, calls=%fused_computation.171 | loop fusion | bytes 18874368 | tf_op jit(solution)/shard_map/slice | solution.py:50
  42.1 1.3 copy-done.10
  43.4 2.2 convert_reduce_fusion
  45.6 1.4 multiply_convert_fusion.2
  49.2 2.8 %collective-permute-start.6 = (bf16[2,1,48,256]{3,2,1,0:T(8,128)(2,1)}, bf16[2,1,48,256]{3,2,1,0:T(8,128)(2,1)}, u32[]{:S(2)}, u32[]{:S(2)}) collective-permute-start(bf16[2,1,48,256]{3,2,1,0:T(8,128)(2,1)} %get-tuple-element.37), channel_id=1, source_target_pairs={{0,8},{1,9},{2,10},{3,11},{4,12},{5,13},{6,14},{7,15},{8,0},{9,1},... | collective-permute-start | bytes 147464 | tf_op jit(solution)/shard_map/ppermute | solution.py:10
  52.3 5.4 %collective-permute-start.7 = (bf16[2,1,48,256]{3,2,1,0:T(8,128)(2,1)}, bf16[2,1,48,256]{3,2,1,0:T(8,128)(2,1)}, u32[]{:S(2)}, u32[]{:S(2)}) collective-permute-start(bf16[2,1,48,256]{3,2,1,0:T(8,128)(2,1)} %get-tuple-element.38), channel_id=1, source_target_pairs={{0,16},{16,32},{32,48},{48,64},{64,80},{80,96},{96,112},{1,17},{17... | collective-permute-start | bytes 147464 | tf_op jit(solution)/shard_map/ppermute | solution.py:20
  57.7 1.3 fusion.21
  59.0 5.2 %reshape.176 = f32[2,16,2,24,2,256]{5,4,3,2,1,0:T(2,128)} reshape(f32[3072,256]{1,0:T(8,128)} %copy-done.4) | data formatting | bytes 6291456 | tf_op jit(solution)/shard_map/reshape | solution.py:56
  64.2 2.8 %fusion.31 = f32[9,256,256]{2,1,0:T(8,128)} fusion(f32[9,256,256]{2,1,0:T(8,128)} %fusion.21, bf16[2,32,48,256]{3,2,1,0:T(8,128)(2,1)S(1)} %multiply_convert_fusion.2, bf16[2,32,48,256]{3,2,1,0:T(8,128)(2,1)} %param.4, bf16[2,1,48,256]{3,2,1,0:T(8,128)(2,1)} %copy-done.14), kind=kOutput, calls=%fused_computation.76 | convolution fusion | flops 405897216 | bytes 3457024 | tf_op jit(solution)/shard_map/dot_general | solution.py:100
  67.1 1.3 fusion.20
  68.4 1.3 fusion.19
  69.8 1.4 fusion.18
  71.3 1.3 fusion.17
  72.6 1.3 fusion.16
  73.9 1.3 fusion.25
  75.2 1.3 fusion.15
  77.3 3.2 %multiply_reduce_fusion = f32[2,16,24,256]{3,2,1,0:T(8,128)S(1)} fusion(f32[16,2]{1,0:T(8,128)S(1)} %add_cosine_fusion, f32[256]{0:T(256)S(1)} %copy-done.18, f32[2,16,2,24,2,256]{5,4,3,2,1,0:T(2,128)} %reshape.176), kind=kLoop, calls=%fused_computation.23 | loop fusion | flops 6881280 | bytes 3933312 | tf_op jit(solution)/shard_map/reduce_sum | solution.py:119
  81.4 72.1 %psum.15 = f32[256]{0:T(256)} all-reduce(f32[256]{0:T(256)S(1)} %copy-done.21), channel_id=1, replica_groups=mesh['lat'=8,'lon'=16] {'lat','lon'}, use_global_device_ids=true, to_apply=%region_3.4 | all-reduce | flops 256 | bytes 2048 | tf_op jit(solution)/shard_map/psum | solution.py:129
  156.3 1.6 collective-permute-start.10
  158.1 1.5 collective-permute-done.11
  163.7 2.1 pad_maximum_fusion.3
  170.5 1.5 convolution_add_fusion.4
  175.5 1.3 pad_maximum_fusion.7
  176.8 57.3 %all-reduce.2.cloned.1.call-done = f32[9,256,256]{2,1,0:T(8,128)} async-done(((f32[9,256,256]{2,1,0:T(8,128)}), f32[9,256,256]{2,1,0:T(8,128)}) %all-reduce.2.cloned.1.call-update) | async-done | bytes 2359312 | tf_op jit(solution)/shard_map/psum | solution.py:129
  234.1 3.2 %copy.45 = f32[9,256,256]{2,1,0:T(8,128)} copy(f32[9,256,256]{2,1,0:T(8,128)} %all-reduce.2.cloned.1.call-done) | data formatting | bytes 4718592
  (117 shorter events, 32.1 us)
Async XLA Ops:
  7.2 226.9 %all-reduce.2.cloned.1.call-start = ((), (), s32[]{:S(2)}) async-start(), calls=%async_computation | async-start | bytes 4718592 | tf_op jit(solution)/shard_map/psum | solution.py:129
  8.0 19.7 %collective-permute-start.2 = (bf16[2,1,48,256]{3,2,1,0:T(8,128)(2,1)S(1)}, bf16[2,1,48,256]{3,2,1,0:T(8,128)(2,1)S(1)}, u32[]{:S(2)}, u32[]{:S(2)}) collective-permute-start(bf16[2,1,48,256]{3,2,1,0:T(8,128)(2,1)S(1)} %get-tuple-element.41), channel_id=1, source_target_pairs={{0,8},{1,9},{2,10},{3,11},{4,12},{5,13},{6,14},{7,15},{8,0},{9,1},... | collective-permute-start | bytes 147464 | tf_op jit(solution)/shard_map/ppermute | solution.py:10
  11.7 16.1 %collective-permute-start.1 = (bf16[2,1,48,256]{3,2,1,0:T(8,128)(2,1)S(1)}, bf16[2,1,48,256]{3,2,1,0:T(8,128)(2,1)S(1)}, u32[]{:S(2)}, u32[]{:S(2)}) collective-permute-start(bf16[2,1,48,256]{3,2,1,0:T(8,128)(2,1)S(1)} %get-tuple-element.41), channel_id=1, source_target_pairs={{0,16},{16,32},{32,48},{48,64},{64,80},{80,96},{96,112},{1,17},{17... | collective-permute-start | bytes 147464 | tf_op jit(solution)/shard_map/ppermute | solution.py:20
  15.2 12.5 %collective-permute-start.3 = (bf16[2,1,48,256]{3,2,1,0:T(8,128)(2,1)S(1)}, bf16[2,1,48,256]{3,2,1,0:T(8,128)(2,1)S(1)}, u32[]{:S(2)}, u32[]{:S(2)}) collective-permute-start(bf16[2,1,48,256]{3,2,1,0:T(8,128)(2,1)S(1)} %get-tuple-element.42), channel_id=1, source_target_pairs={{16,0},{32,16},{48,32},{64,48},{80,64},{96,80},{112,96},{17,1},{33... | collective-permute-start | bytes 147464 | tf_op jit(solution)/shard_map/ppermute | solution.py:21
  16.5 11.3 %collective-permute-start = (bf16[2,1,48,256]{3,2,1,0:T(8,128)(2,1)S(1)}, bf16[2,1,48,256]{3,2,1,0:T(8,128)(2,1)S(1)}, u32[]{:S(2)}, u32[]{:S(2)}) collective-permute-start(bf16[2,1,48,256]{3,2,1,0:T(8,128)(2,1)S(1)} %get-tuple-element.42), channel_id=1, source_target_pairs={{0,8},{1,9},{2,10},{3,11},{4,12},{5,13},{6,14},{7,15},{8,0},{9,1},... | collective-permute-start | bytes 147464 | tf_op jit(solution)/shard_map/ppermute | solution.py:10
  17.1 1.4 copy-start.19
  17.3 9.9 %copy-start.15 = (f32[32]{0:T(128)}, f32[32]{0:T(128)S(1)}, u32[]{:S(2)}) copy-start(f32[32]{0:T(128)S(1)} %fusion.97) | copy-start | bytes 388
  27.1 1.4 copy-start
  27.8 5.9 %copy-start.12 = (bf16[2,1,48,256]{3,2,1,0:T(8,128)(2,1)}, bf16[2,1,48,256]{3,2,1,0:T(8,128)(2,1)S(1)}, u32[]{:S(2)}) copy-start(bf16[2,1,48,256]{3,2,1,0:T(8,128)(2,1)S(1)} %broadcast_select_fusion.1) | copy-start | bytes 147460
  28.5 5.2 %copy-start.14 = (bf16[2,1,48,256]{3,2,1,0:T(8,128)(2,1)}, bf16[2,1,48,256]{3,2,1,0:T(8,128)(2,1)S(1)}, u32[]{:S(2)}) copy-start(bf16[2,1,48,256]{3,2,1,0:T(8,128)(2,1)S(1)} %broadcast_select_fusion.3) | copy-start | bytes 147460
  28.6 3.3 %copy-start.8 = (bf16[9,256,256]{2,1,0:T(8,128)(2,1)S(1)}, bf16[9,256,256]{2,1,0:T(8,128)(2,1)}, u32[]{:S(2)}) copy-start(bf16[9,256,256]{2,1,0:T(8,128)(2,1)} %param.5) | copy-start | bytes 3538948
  28.8 4.8 %collective-permute-start.5 = (bf16[2,34,1,256]{3,2,1,0:T(2,128)(2,1)S(1)}, bf16[2,34,1,256]{3,2,1,0:T(2,128)(2,1)S(1)}, u32[]{:S(2)}, u32[]{:S(2)}) collective-permute-start(bf16[2,34,1,256]{3,2,1,0:T(2,128)(2,1)S(1)} %get-tuple-element.35), channel_id=1, source_target_pairs={{1,0},{2,1},{3,2},{4,3},{5,4},{6,5},{7,6},{8,7},{9,8},{10,9},{11,1... | collective-permute-start | bytes 104456 | tf_op jit(solution)/shard_map/ppermute | solution.py:21
  30.4 3.3 %collective-permute-start.4 = (bf16[2,34,1,256]{3,2,1,0:T(2,128)(2,1)S(1)}, bf16[2,34,1,256]{3,2,1,0:T(2,128)(2,1)S(1)}, u32[]{:S(2)}, u32[]{:S(2)}) collective-permute-start(bf16[2,34,1,256]{3,2,1,0:T(2,128)(2,1)S(1)} %get-tuple-element.36), channel_id=1, source_target_pairs={{0,1},{1,2},{2,3},{3,4},{4,5},{5,6},{6,7},{7,8},{8,9},{9,10},{10,1... | collective-permute-start | bytes 104456 | tf_op jit(solution)/shard_map/ppermute | solution.py:20
  34.9 3.1 %copy-start.2 = (bf16[2,34,49,256]{3,2,1,0:T(8,128)(2,1)}, bf16[2,34,49,256]{3,2,1,0:T(8,128)(2,1)S(1)}, u32[]{:S(2)}) copy-start(bf16[2,34,49,256]{3,2,1,0:T(8,128)(2,1)S(1)} %get-tuple-element.33) | copy-start | bytes 5117956
  41.5 1.9 copy-start.10
  41.5 1.9 copy-start.17
  43.4 2.2 copy-start.6
  43.4 2.2 copy-start.16
  45.6 1.7 copy-start.4
  48.0 106.5 %collective-permute-start.9 = (bf16[2,1,48,256]{3,2,1,0:T(8,128)(2,1)}, bf16[2,1,48,256]{3,2,1,0:T(8,128)(2,1)}, u32[]{:S(2)}, u32[]{:S(2)}) collective-permute-start(bf16[2,1,48,256]{3,2,1,0:T(8,128)(2,1)} %get-tuple-element.37), channel_id=1, source_target_pairs={{16,0},{32,16},{48,32},{64,48},{80,64},{96,80},{112,96},{17,1},{33... | collective-permute-start | bytes 147464 | tf_op jit(solution)/shard_map/ppermute | solution.py:21
  49.2 104.2 %collective-permute-start.6 = (bf16[2,1,48,256]{3,2,1,0:T(8,128)(2,1)}, bf16[2,1,48,256]{3,2,1,0:T(8,128)(2,1)}, u32[]{:S(2)}, u32[]{:S(2)}) collective-permute-start(bf16[2,1,48,256]{3,2,1,0:T(8,128)(2,1)} %get-tuple-element.37), channel_id=1, source_target_pairs={{0,8},{1,9},{2,10},{3,11},{4,12},{5,13},{6,14},{7,15},{8,0},{9,1},... | collective-permute-start | bytes 147464 | tf_op jit(solution)/shard_map/ppermute | solution.py:10
  52.1 102.4 %collective-permute-start.8 = (bf16[2,1,48,256]{3,2,1,0:T(8,128)(2,1)}, bf16[2,1,48,256]{3,2,1,0:T(8,128)(2,1)}, u32[]{:S(2)}, u32[]{:S(2)}) collective-permute-start(bf16[2,1,48,256]{3,2,1,0:T(8,128)(2,1)} %get-tuple-element.38), channel_id=1, source_target_pairs={{0,8},{1,9},{2,10},{3,11},{4,12},{5,13},{6,14},{7,15},{8,0},{9,1},... | collective-permute-start | bytes 147464 | tf_op jit(solution)/shard_map/ppermute | solution.py:10
  52.3 101.2 %collective-permute-start.7 = (bf16[2,1,48,256]{3,2,1,0:T(8,128)(2,1)}, bf16[2,1,48,256]{3,2,1,0:T(8,128)(2,1)}, u32[]{:S(2)}, u32[]{:S(2)}) collective-permute-start(bf16[2,1,48,256]{3,2,1,0:T(8,128)(2,1)} %get-tuple-element.38), channel_id=1, source_target_pairs={{0,16},{16,32},{32,48},{48,64},{64,80},{80,96},{96,112},{1,17},{17... | collective-permute-start | bytes 147464 | tf_op jit(solution)/shard_map/ppermute | solution.py:20
  64.2 2.9 %copy-start.3 = (bf16[2,34,49,256]{3,2,1,0:T(8,128)(2,1)S(1)}, bf16[2,34,49,256]{3,2,1,0:T(8,128)(2,1)}, u32[]{:S(2)}) copy-start(bf16[2,34,49,256]{3,2,1,0:T(8,128)(2,1)} %copy-done.2) | copy-start | bytes 5117956
  77.3 3.2 %copy-start.20 = (f32[16]{0:T(128)S(1)}, f32[16]{0:T(128)}, u32[]{:S(2)}) copy-start(f32[16]{0:T(128)} %copy-done.19) | copy-start | bytes 196
  77.3 4.1 %copy-start.21 = (f32[256]{0:T(256)S(1)}, f32[256]{0:T(256)}, u32[]{:S(2)}) copy-start(f32[256]{0:T(256)} %get-tuple-element.43) | copy-start | bytes 3076
  77.3 77.0 %copy-start.9 = (bf16[9,256,256]{2,1,0:T(8,128)(2,1)S(1)}, bf16[9,256,256]{2,1,0:T(8,128)(2,1)}, u32[]{:S(2)}) copy-start(bf16[9,256,256]{2,1,0:T(8,128)(2,1)} %param.5) | copy-start | bytes 3538948
  155.4 4.1 %collective-permute-start.11 = (bf16[2,34,1,256]{3,2,1,0:T(2,128)(2,1)S(1)}, bf16[2,34,1,256]{3,2,1,0:T(2,128)(2,1)S(1)}, u32[]{:S(2)}, u32[]{:S(2)}) collective-permute-start(bf16[2,34,1,256]{3,2,1,0:T(2,128)(2,1)S(1)} %get-tuple-element.31), channel_id=1, source_target_pairs={{1,0},{2,1},{3,2},{4,3},{5,4},{6,5},{7,6},{8,7},{9,8},{10,9},{11,1... | collective-permute-start | bytes 104456 | tf_op jit(solution)/shard_map/ppermute | solution.py:21
  156.3 3.3 %collective-permute-start.10 = (bf16[2,34,1,256]{3,2,1,0:T(2,128)(2,1)S(1)}, bf16[2,34,1,256]{3,2,1,0:T(2,128)(2,1)S(1)}, u32[]{:S(2)}, u32[]{:S(2)}) collective-permute-start(bf16[2,34,1,256]{3,2,1,0:T(2,128)(2,1)S(1)} %get-tuple-element.32), channel_id=1, source_target_pairs={{0,1},{1,2},{2,3},{3,4},{4,5},{5,6},{6,7},{7,8},{8,9},{9,10},{10,1... | collective-permute-start | bytes 104456 | tf_op jit(solution)/shard_map/ppermute | solution.py:20
  162.2 1.5 slice-start
  167.6 1.9 copy-start.5
  167.6 2.8 %copy-start.11 = (f32[3072,256]{1,0:T(8,128)S(1)}, f32[3072,256]{1,0:T(8,128)}, u32[]{:S(2)}) copy-start(f32[3072,256]{1,0:T(8,128)} %reshape.184) | copy-start | bytes 9437188
  (4 other events, 4.7 us)
Sparse Core Ops, SparseCore 0:
  76.7 157.3 all-reduce.1
where the time goes:
time: 245 us; the launch traced here: 244 us
  blocking collectives  72.1 us (29%)
  waiting for transfers between devices  60.1 us (25%)
  local copies, waits for them, and re-layouts  30.9 us (13%)
  matrix products  27.7 us (11%)
  starting transfers between devices  24.1 us (10%)
  other arithmetic  14.8 us (6%)
  between operations  14.5 us (6%)
    psum x1, blocking collectives, local(): grad_kernel, grad_bias = lax.psum((kernel_part, bias_part), ('lat', 'lon'))  72.1 us
    psum x1, waiting for transfers between devices, local(): grad_kernel, grad_bias = lax.psum((kernel_part, bias_part), ('lat', 'lon'))  57.3 us
    dot_general x9, matrix products, kernel_grad(): lax.dot_general(window, flat_grad, (((0,), (0,)), ((), ())), preferred_el...  13.5 us
    ppermute x4, starting transfers between devices, with_halo(): before = lax.ppermute(last, axis, up)  12 us
    unnamed x45, local copies, waits for them, and re-layouts  8.65 us
    ppermute x4, starting transfers between devices, shifted(): lax.ppermute(shard, axis, [(i, (i + by) % size) for i in range(size)])  6.98 us
    reshape x2, local copies, waits for them, and re-layouts, local(): jnp.repeat(jnp.repeat(cotangent.astype(jnp.float32), 2, axis=1), 2, axis=2)  6.82 us
    dot_general x9, matrix products, forward_conv(): jnp.dot(window, kernel[3 * row_off + col_off], preferred_element_type=jnp...  6.79 us
  transfers between devices with their start and end apart: 13, of which 4 were waited for; matrix products, arithmetic and copies ran while one was open for 21% of the time, Pallas kernels for 0%

commit v1 on v0

--- a/solution.py
+++ b/solution.py
@@ -126,7 +126,12 @@
     )
     kernel_part = kernel_grad(padded, grad_pre, rows, cols)
     bias_part = jnp.sum(grad_pre.astype(jnp.float32), axis=(0, 1, 2))
-    grad_kernel, grad_bias = lax.psum((kernel_part, bias_part), ("lat", "lon"))
+
+    def switch_the_roads(z_in):
+        piece_out = jax.lax.psum(z_in, "lat")
+        return jax.lax.psum(piece_out, "lon")
+
+    grad_kernel, grad_bias = switch_the_roads((kernel_part, bias_part))
     grad_padded = extend(grad_pre)
     is_north = lat_place == 0
     is_south = lat_place == lat_count - 1

time: 245 us -> 312 us (1.27)
  waiting for transfers between devices: 60.1 us -> 136 us
  blocking collectives: 72.1 us -> 56.8 us
  matrix products: 27.7 us -> 31.9 us
    psum x1 -> x2, waiting for transfers between devices: 57.3 us -> 132 us  [the longest x1 123 us: switch_the_roads(): return jax.lax.psum(piece_out, 'lon')]
    psum x1 -> x2, blocking collectives: 72.1 us -> 56.8 us  [the longest x1 36.5 us: switch_the_roads(): return jax.lax.psum(piece_out, 'lon')]
    dot_general x9, matrix products: 6.33 us -> 10.5 us  [back_conv(): lax.dot_general(window, kernel[3 * row_off + col_off], (((1,), (1,)), (()...]
    unnamed x45 -> x49, local copies, waits for them, and re-layouts: 8.65 us -> 9.38 us
  transfers between devices with their start and end apart: 13 -> 14, of which waited for: 4 -> 5; matrix products, arithmetic and copies ran while one was open for 21% -> 18% of each run, Pallas kernels for 0% -> 0%
where the time goes in v1:
time: 312 us
  waiting for transfers between devices  136 us (44%)
  blocking collectives  56.8 us (18%)
  matrix products  31.9 us (10%)
  local copies, waits for them, and re-layouts  31.6 us (10%)
  starting transfers between devices  23.4 us (8%)
  other arithmetic  17.1 us (5%)
  between operations  14.5 us (5%)
    psum x1, waiting for transfers between devices, switch_the_roads(): return jax.lax.psum(piece_out, 'lon')  123 us
    psum x1, blocking collectives, switch_the_roads(): return jax.lax.psum(piece_out, 'lon')  36.5 us
    psum x1, blocking collectives, switch_the_roads(): piece_out = jax.lax.psum(z_in, 'lat')  20.3 us
    dot_general x9, matrix products, kernel_grad(): lax.dot_general(window, flat_grad, (((0,), (0,)), ((), ())), preferred_el...  13.5 us
    ppermute x4, starting transfers between devices, with_halo(): before = lax.ppermute(last, axis, up)  11.4 us
    dot_general x9, matrix products, back_conv(): lax.dot_general(window, kernel[3 * row_off + col_off], (((1,), (1,)), (()...  10.5 us
    unnamed x49, local copies, waits for them, and re-layouts  9.38 us
    psum x1, waiting for transfers between devices, switch_the_roads(): piece_out = jax.lax.psum(z_in, 'lat')  9.15 us
  transfers between devices with their start and end apart: 14, of which 5 were waited for; matrix products, arithmetic and copies ran while one was open for 18% of the time, Pallas kernels for 0%

profile of v1, /device:TPU:1, one launch (start us, length us, event | category | flops | bytes accessed | tf_op | source)
XLA Modules:
  0.0 311.6 jit_solution(14044216192749639522)
XLA Ops:
  8.0 3.6 %collective-permute-start.2 = (bf16[2,1,48,256]{3,2,1,0:T(8,128)(2,1)S(1)}, bf16[2,1,48,256]{3,2,1,0:T(8,128)(2,1)S(1)}, u32[]{:S(2)}, u32[]{:S(2)}) collective-permute-start(bf16[2,1,48,256]{3,2,1,0:T(8,128)(2,1)S(1)} %get-tuple-element.41), channel_id=1, source_target_pairs={{0,8},{1,9},{2,10},{3,11},{4,12},{5,13},{6,14},{7,15},{8,0},{9,1},... | collective-permute-start | bytes 147464 | tf_op jit(solution)/shard_map/ppermute | solution.py:10
  11.7 3.5 %collective-permute-start.1 = (bf16[2,1,48,256]{3,2,1,0:T(8,128)(2,1)S(1)}, bf16[2,1,48,256]{3,2,1,0:T(8,128)(2,1)S(1)}, u32[]{:S(2)}, u32[]{:S(2)}) collective-permute-start(bf16[2,1,48,256]{3,2,1,0:T(8,128)(2,1)S(1)} %get-tuple-element.41), channel_id=1, source_target_pairs={{0,16},{16,32},{32,48},{48,64},{64,80},{80,96},{96,112},{1,17},{17... | collective-permute-start | bytes 147464 | tf_op jit(solution)/shard_map/ppermute | solution.py:20
  18.5 1.7 broadcast_in_dim.22
  20.3 3.4 %reshape.184 = f32[3072,256]{1,0:T(8,128)} reshape(f32[2,32,24,2,256]{4,3,2,1,0:T(2,128)S(1)} %broadcast_in_dim.22) | data formatting | bytes 6291456 | tf_op jit(solution)/shard_map/reshape | solution.py:123
  23.7 3.4 %reshape.178 = f32[2,32,48,256]{3,2,1,0:T(8,128)} reshape(f32[2,32,24,2,256]{4,3,2,1,0:T(2,128)S(1)} %broadcast_in_dim.22) | data formatting | bytes 6291456 | tf_op jit(solution)/shard_map/reshape | solution.py:123
  28.8 1.6 collective-permute-start.5
  30.4 1.4 collective-permute-start.4
  34.9 3.1 fusion.104
  43.4 2.2 convert_reduce_fusion
  45.6 1.4 multiply_convert_fusion.2
  49.2 2.8 collective-permute-start.6
  52.3 5.4 %collective-permute-start.7 = (bf16[2,1,48,256]{3,2,1,0:T(8,128)(2,1)}, bf16[2,1,48,256]{3,2,1,0:T(8,128)(2,1)}, u32[]{:S(2)}, u32[]{:S(2)}) collective-permute-start(bf16[2,1,48,256]{3,2,1,0:T(8,128)(2,1)} %get-tuple-element.38), channel_id=1, source_target_pairs={{0,16},{16,32},{32,48},{48,64},{64,80},{80,96},{96,112},{1,17},{17... | collective-permute-start | bytes 147464 | tf_op jit(solution)/shard_map/ppermute | solution.py:20
  59.0 5.2 %reshape.176 = f32[2,16,2,24,2,256]{5,4,3,2,1,0:T(2,128)} reshape(f32[3072,256]{1,0:T(8,128)} %copy-done.4) | data formatting | bytes 6291456 | tf_op jit(solution)/shard_map/reshape | solution.py:56
  64.2 2.8 fusion.31
  67.1 1.3 fusion.20
  69.8 1.4 fusion.18
  71.3 1.3 fusion.17
  72.6 1.3 fusion.16
  73.9 1.3 fusion.25
  75.3 1.3 fusion.15
  77.3 3.1 %multiply_reduce_fusion = f32[2,16,24,256]{3,2,1,0:T(8,128)S(1)} fusion(f32[16,2]{1,0:T(8,128)S(1)} %add_cosine_fusion, f32[256]{0:T(256)S(1)} %copy-done.20, f32[2,16,2,24,2,256]{5,4,3,2,1,0:T(2,128)} %reshape.176), kind=kLoop, calls=%fused_computation.23 | loop fusion | flops 6881280 | bytes 3933312 | tf_op jit(solution)/shard_map/reduce_sum | solution.py:119
  81.3 20.3 %psum.30 = f32[256]{0:T(256)S(1)} all-reduce(f32[256]{0:T(256)S(1)} %copy-done.23), channel_id=1, replica_groups=mesh['lat'=8,'lon'=16] {'lat'}, use_global_device_ids=true, to_apply=%region_4.5 | all-reduce | flops 256 | bytes 2048 | tf_op jit(solution)/shard_map/psum | solution.py:131
  101.5 36.5 %psum.31 = f32[256]{0:T(256)} all-reduce(f32[256]{0:T(256)S(1)} %psum.30), channel_id=1, replica_groups=mesh['lat'=8,'lon'=16] {'lon'}, use_global_device_ids=true, to_apply=%region_5.6 | all-reduce | flops 256 | bytes 2048 | tf_op jit(solution)/shard_map/psum | solution.py:132
  142.0 3.1 %collective-permute-done.11 = bf16[2,34,1,256]{3,2,1,0:T(2,128)(2,1)S(1)} collective-permute-done((bf16[2,34,1,256]{3,2,1,0:T(2,128)(2,1)S(1)}, bf16[2,34,1,256]{3,2,1,0:T(2,128)(2,1)S(1)}, u32[]{:S(2)}, u32[]{:S(2)}) %collective-permute-start.11) | collective-permute-done | bytes 34848 | tf_op jit(solution)/shard_map/ppermute | solution.py:21
  149.3 4.5 %pad_maximum_fusion.3 = (bf16[2,32,48,256]{3,2,1,0:T(8,128)(2,1)}, bf16[2,32,48,256]{3,2,1,0:T(8,128)(2,1)}, bf16[2,32,48,256]{3,2,1,0:T(8,128)(2,1)}, bf16[2,32...) fusion(bf16[2,32,50,256]{3,2,1,0:T(8,128)(2,1)S(1)} %slice-done, ...), kind=kLoop, calls=%fused_computation.51 | loop fusion | flops 18874368 | bytes 11177984 | tf_op jit(solution)/shard_map/concatenate | solution.py:141
  158.5 1.5 convolution_add_fusion.4
  159.9 2.2 convolution_add_fusion.3
  162.2 9.2 %all-reduce.3.cloned.1.call-done = f32[9,256,256]{2,1,0:T(8,128)} async-done(((f32[9,256,256]{2,1,0:T(8,128)}), f32[9,256,256]{2,1,0:T(8,128)}) %all-reduce.3.cloned.1.call-update) | async-done | bytes 2359312 | tf_op jit(solution)/shard_map/psum | solution.py:131
  171.4 3.1 convolution_add_fusion.2
  177.6 1.3 pad_maximum_fusion.7
  178.9 122.6 %all-reduce.5.cloned.1.call-done = f32[9,256,256]{2,1,0:T(8,128)} async-done(((f32[9,256,256]{2,1,0:T(8,128)}), f32[9,256,256]{2,1,0:T(8,128)}) %all-reduce.5.cloned.1.call-update) | async-done | bytes 2359312 | tf_op jit(solution)/shard_map/psum | solution.py:132
  301.6 3.2 %copy.46 = f32[9,256,256]{2,1,0:T(8,128)} copy(f32[9,256,256]{2,1,0:T(8,128)} %all-reduce.5.cloned.1.call-done) | data formatting | bytes 4718592
  (125 shorter events, 36.6 us)
Async XLA Ops:
  7.2 164.2 %all-reduce.3.cloned.1.call-start = ((), (), s32[]{:S(2)}) async-start(), calls=%async_computation | async-start | bytes 4718592 | tf_op jit(solution)/shard_map/psum | solution.py:131
  8.0 19.7 %collective-permute-start.2 = (bf16[2,1,48,256]{3,2,1,0:T(8,128)(2,1)S(1)}, bf16[2,1,48,256]{3,2,1,0:T(8,128)(2,1)S(1)}, u32[]{:S(2)}, u32[]{:S(2)}) collective-permute-start(bf16[2,1,48,256]{3,2,1,0:T(8,128)(2,1)S(1)} %get-tuple-element.41), channel_id=1, source_target_pairs={{0,8},{1,9},{2,10},{3,11},{4,12},{5,13},{6,14},{7,15},{8,0},{9,1},... | collective-permute-start | bytes 147464 | tf_op jit(solution)/shard_map/ppermute | solution.py:10
  11.7 16.1 %collective-permute-start.1 = (bf16[2,1,48,256]{3,2,1,0:T(8,128)(2,1)S(1)}, bf16[2,1,48,256]{3,2,1,0:T(8,128)(2,1)S(1)}, u32[]{:S(2)}, u32[]{:S(2)}) collective-permute-start(bf16[2,1,48,256]{3,2,1,0:T(8,128)(2,1)S(1)} %get-tuple-element.41), channel_id=1, source_target_pairs={{0,16},{16,32},{32,48},{48,64},{64,80},{80,96},{96,112},{1,17},{17... | collective-permute-start | bytes 147464 | tf_op jit(solution)/shard_map/ppermute | solution.py:20
  15.2 12.5 %collective-permute-start.3 = (bf16[2,1,48,256]{3,2,1,0:T(8,128)(2,1)S(1)}, bf16[2,1,48,256]{3,2,1,0:T(8,128)(2,1)S(1)}, u32[]{:S(2)}, u32[]{:S(2)}) collective-permute-start(bf16[2,1,48,256]{3,2,1,0:T(8,128)(2,1)S(1)} %get-tuple-element.42), channel_id=1, source_target_pairs={{16,0},{32,16},{48,32},{64,48},{80,64},{96,80},{112,96},{17,1},{33... | collective-permute-start | bytes 147464 | tf_op jit(solution)/shard_map/ppermute | solution.py:21
  16.5 11.3 %collective-permute-start = (bf16[2,1,48,256]{3,2,1,0:T(8,128)(2,1)S(1)}, bf16[2,1,48,256]{3,2,1,0:T(8,128)(2,1)S(1)}, u32[]{:S(2)}, u32[]{:S(2)}) collective-permute-start(bf16[2,1,48,256]{3,2,1,0:T(8,128)(2,1)S(1)} %get-tuple-element.42), channel_id=1, source_target_pairs={{0,8},{1,9},{2,10},{3,11},{4,12},{5,13},{6,14},{7,15},{8,0},{9,1},... | collective-permute-start | bytes 147464 | tf_op jit(solution)/shard_map/ppermute | solution.py:10
  17.3 9.9 %copy-start.17 = (f32[32]{0:T(128)}, f32[32]{0:T(128)S(1)}, u32[]{:S(2)}) copy-start(f32[32]{0:T(128)S(1)} %fusion.97) | copy-start | bytes 388
  27.8 5.9 %copy-start.14 = (bf16[2,1,48,256]{3,2,1,0:T(8,128)(2,1)}, bf16[2,1,48,256]{3,2,1,0:T(8,128)(2,1)S(1)}, u32[]{:S(2)}) copy-start(bf16[2,1,48,256]{3,2,1,0:T(8,128)(2,1)S(1)} %broadcast_select_fusion.1) | copy-start | bytes 147460
  28.5 5.2 %copy-start.16 = (bf16[2,1,48,256]{3,2,1,0:T(8,128)(2,1)}, bf16[2,1,48,256]{3,2,1,0:T(8,128)(2,1)S(1)}, u32[]{:S(2)}) copy-start(bf16[2,1,48,256]{3,2,1,0:T(8,128)(2,1)S(1)} %broadcast_select_fusion.3) | copy-start | bytes 147460
  28.6 3.3 %copy-start.8 = (bf16[9,256,256]{2,1,0:T(8,128)(2,1)S(1)}, bf16[9,256,256]{2,1,0:T(8,128)(2,1)}, u32[]{:S(2)}) copy-start(bf16[9,256,256]{2,1,0:T(8,128)(2,1)} %param.5) | copy-start | bytes 3538948
  28.8 4.8 %collective-permute-start.5 = (bf16[2,34,1,256]{3,2,1,0:T(2,128)(2,1)S(1)}, bf16[2,34,1,256]{3,2,1,0:T(2,128)(2,1)S(1)}, u32[]{:S(2)}, u32[]{:S(2)}) collective-permute-start(bf16[2,34,1,256]{3,2,1,0:T(2,128)(2,1)S(1)} %get-tuple-element.35), channel_id=1, source_target_pairs={{1,0},{2,1},{3,2},{4,3},{5,4},{6,5},{7,6},{8,7},{9,8},{10,9},{11,1... | collective-permute-start | bytes 104456 | tf_op jit(solution)/shard_map/ppermute | solution.py:21
  30.4 3.3 %collective-permute-start.4 = (bf16[2,34,1,256]{3,2,1,0:T(2,128)(2,1)S(1)}, bf16[2,34,1,256]{3,2,1,0:T(2,128)(2,1)S(1)}, u32[]{:S(2)}, u32[]{:S(2)}) collective-permute-start(bf16[2,34,1,256]{3,2,1,0:T(2,128)(2,1)S(1)} %get-tuple-element.36), channel_id=1, source_target_pairs={{0,1},{1,2},{2,3},{3,4},{4,5},{5,6},{6,7},{7,8},{8,9},{9,10},{10,1... | collective-permute-start | bytes 104456 | tf_op jit(solution)/shard_map/ppermute | solution.py:20
  34.9 3.1 %copy-start.2 = (bf16[2,34,49,256]{3,2,1,0:T(8,128)(2,1)}, bf16[2,34,49,256]{3,2,1,0:T(8,128)(2,1)S(1)}, u32[]{:S(2)}) copy-start(bf16[2,34,49,256]{3,2,1,0:T(8,128)(2,1)S(1)} %get-tuple-element.33) | copy-start | bytes 5117956
  41.5 1.9 copy-start.12
  41.5 1.9 copy-start.19
  43.4 2.2 copy-start.6
  43.4 2.2 copy-start.18
  45.6 1.7 copy-start.4
  48.0 91.1 %collective-permute-start.9 = (bf16[2,1,48,256]{3,2,1,0:T(8,128)(2,1)}, bf16[2,1,48,256]{3,2,1,0:T(8,128)(2,1)}, u32[]{:S(2)}, u32[]{:S(2)}) collective-permute-start(bf16[2,1,48,256]{3,2,1,0:T(8,128)(2,1)} %get-tuple-element.37), channel_id=1, source_target_pairs={{16,0},{32,16},{48,32},{64,48},{80,64},{96,80},{112,96},{17,1},{33... | collective-permute-start | bytes 147464 | tf_op jit(solution)/shard_map/ppermute | solution.py:21
  49.2 88.8 %collective-permute-start.6 = (bf16[2,1,48,256]{3,2,1,0:T(8,128)(2,1)}, bf16[2,1,48,256]{3,2,1,0:T(8,128)(2,1)}, u32[]{:S(2)}, u32[]{:S(2)}) collective-permute-start(bf16[2,1,48,256]{3,2,1,0:T(8,128)(2,1)} %get-tuple-element.37), channel_id=1, source_target_pairs={{0,8},{1,9},{2,10},{3,11},{4,12},{5,13},{6,14},{7,15},{8,0},{9,1},... | collective-permute-start | bytes 147464 | tf_op jit(solution)/shard_map/ppermute | solution.py:10
  52.1 87.0 %collective-permute-start.8 = (bf16[2,1,48,256]{3,2,1,0:T(8,128)(2,1)}, bf16[2,1,48,256]{3,2,1,0:T(8,128)(2,1)}, u32[]{:S(2)}, u32[]{:S(2)}) collective-permute-start(bf16[2,1,48,256]{3,2,1,0:T(8,128)(2,1)} %get-tuple-element.38), channel_id=1, source_target_pairs={{0,8},{1,9},{2,10},{3,11},{4,12},{5,13},{6,14},{7,15},{8,0},{9,1},... | collective-permute-start | bytes 147464 | tf_op jit(solution)/shard_map/ppermute | solution.py:10
  52.3 85.8 %collective-permute-start.7 = (bf16[2,1,48,256]{3,2,1,0:T(8,128)(2,1)}, bf16[2,1,48,256]{3,2,1,0:T(8,128)(2,1)}, u32[]{:S(2)}, u32[]{:S(2)}) collective-permute-start(bf16[2,1,48,256]{3,2,1,0:T(8,128)(2,1)} %get-tuple-element.38), channel_id=1, source_target_pairs={{0,16},{16,32},{32,48},{48,64},{64,80},{80,96},{96,112},{1,17},{17... | collective-permute-start | bytes 147464 | tf_op jit(solution)/shard_map/ppermute | solution.py:20
  64.2 2.8 copy-start.3
  76.6 3.8 %copy-start.22 = (f32[16]{0:T(128)S(1)}, f32[16]{0:T(128)}, u32[]{:S(2)}) copy-start(f32[16]{0:T(128)} %copy-done.21) | copy-start | bytes 196
  76.6 4.7 %copy-start.23 = (f32[256]{0:T(256)S(1)}, f32[256]{0:T(256)}, u32[]{:S(2)}) copy-start(f32[256]{0:T(256)} %get-tuple-element.43) | copy-start | bytes 3076
  76.6 62.3 %copy-start.9 = (bf16[9,256,256]{2,1,0:T(8,128)(2,1)S(1)}, bf16[9,256,256]{2,1,0:T(8,128)(2,1)}, u32[]{:S(2)}) copy-start(bf16[9,256,256]{2,1,0:T(8,128)(2,1)} %param.5) | copy-start | bytes 3538948
  76.7 224.9 %all-reduce.5.cloned.1.call-start = ((), (), s32[]{:S(2)}) async-start(), calls=%async_computation.1 | async-start | bytes 4718592 | tf_op jit(solution)/shard_map/psum | solution.py:132
  140.1 5.1 %collective-permute-start.11 = (bf16[2,34,1,256]{3,2,1,0:T(2,128)(2,1)S(1)}, bf16[2,34,1,256]{3,2,1,0:T(2,128)(2,1)S(1)}, u32[]{:S(2)}, u32[]{:S(2)}) collective-permute-start(bf16[2,34,1,256]{3,2,1,0:T(2,128)(2,1)S(1)} %get-tuple-element.31), channel_id=1, source_target_pairs={{1,0},{2,1},{3,2},{4,3},{5,4},{6,5},{7,6},{8,7},{9,8},{10,9},{11,1... | collective-permute-start | bytes 104456 | tf_op jit(solution)/shard_map/ppermute | solution.py:21
  140.9 4.3 %collective-permute-start.10 = (bf16[2,34,1,256]{3,2,1,0:T(2,128)(2,1)S(1)}, bf16[2,34,1,256]{3,2,1,0:T(2,128)(2,1)S(1)}, u32[]{:S(2)}, u32[]{:S(2)}) collective-permute-start(bf16[2,34,1,256]{3,2,1,0:T(2,128)(2,1)S(1)} %get-tuple-element.32), channel_id=1, source_target_pairs={{0,1},{1,2},{2,3},{3,4},{4,5},{5,6},{6,7},{7,8},{8,9},{9,10},{10,1... | collective-permute-start | bytes 104456 | tf_op jit(solution)/shard_map/ppermute | solution.py:20
  147.8 1.5 slice-start
  155.6 1.9 copy-start.5
  155.6 2.9 copy-start.13
  171.3 3.1 copy-start.11
  (7 other events, 9.0 us)
Sparse Core Ops, SparseCore 0:
  76.7 94.5 all-reduce.2
  173.8 127.6 all-reduce.4
